TPU v7x, 512 devices: a whole 4x4x16 slice. The times are simulated.
512 devices in a mesh: gx: 32 (over z, y_lo), gy: 16 (over y_hi, x, core).
Axes of the slice: x: 4, y: 4 (y_hi: 2, y_lo: 2; y = y_hi * 2 + y_lo), z: 16, core: 2. Of those that a mesh axis runs over, the one named last changes fastest.
Arguments:
- fields: float32 [5, 4, 1024, 2048], P(None, None, 'gx', 'gy'), may hold values from -6 to 6
- viscosity: float32 [4, 1024, 2048], P(None, 'gx', 'gy'), may hold values from 0.03 to 0.3
- precursor: float32 [5, 4, 512], P(None, None, 'gy'), may hold values from -6 to 6
- tile_index: int32 [2048], P('gy'), may hold values from 0 to 511, as said below
- fine_fields: float32 [8192, 5, 4, 4, 256], P(('gx', 'gy')), may hold values from -6 to 6
- fine_viscosity: float32 [8192, 4, 4, 256], P(('gx', 'gy')), may hold values from 0.03 to 0.3
- partner_gx: int32 [8192], P(('gx', 'gy')), may hold values from 0 to 31, as said below
- partner_col: int32 [8192], P(('gx', 'gy')), may hold values from 0 to 31
Outputs:
- fields_out: float32 [5, 4, 1024, 2048], P(None, None, 'gx', 'gy')
- fine_out: float32 [8192, 5, 4, 4, 256], P(('gx', 'gy'))
Inputs may be any that keep to these rules, and one draw needn't show every extreme that they name: `tile_index`: inlet cell y takes precursor cell (y + s) mod 512, where s is drawn for each aligned block of 128 cells. `partner_gx`: each device's tiles are glued to outer devices of its own gy row: exactly 2 tiles to each of 8 distinct gx indices; in every gy row one gx index receives 2 tiles from every device of the row.
All inputs are finite; a program needn't handle non-finite values.
Results may differ from a plain program's by a relative error of at most 0.00005.
Values sent between devices are 32-bit elements; how exact they have to be, the bound alone decides.
No kernel may reach another device: no remote copies, remote signals or barrier semaphores. Data moves between devices by JAX's collectives and lax.ppermute only.
A program may use at most 64 MiB of HBM per device.

v0:
```python
import jax
import jax.numpy as jnp
from jax import lax
from jax.sharding import PartitionSpec as P

CAP = 2
time_step = 0.2
vertical_mix = 0.1
coarse_penalty = 0.5
fine_penalty = 1.0


def padded_2(cells, sides, width):
    for axis, dim in sides:
        count = lax.axis_size(axis)
        head = lax.slice_in_dim(cells, 0, width, axis=dim)
        tail = lax.slice_in_dim(cells, cells.shape[dim] - width, cells.shape[dim], axis=dim)
        cells = jnp.concatenate(
            [
                lax.ppermute(tail, axis, [(i, (i + 1) % count) for i in range(count)]),
                cells,
                lax.ppermute(head, axis, [((i + 1) % count, i) for i in range(count)]),
            ],
            axis=dim,
        )
    return cells


def tendency(padded, spacing):
    nfield = padded.shape[-4] - 1
    state_part = padded[..., :nfield, :, :, :]
    visc_part = padded[..., nfield:, :, :, :]
    centre = state_part[..., 1:-1, 1:-1]
    q_east = state_part[..., 2:, 1:-1]
    q_west = state_part[..., :-2, 1:-1]
    q_north = state_part[..., 1:-1, 2:]
    q_south = state_part[..., 1:-1, :-2]
    u_flow = centre[..., 0:1, :, :, :]
    v_flow = centre[..., 1:2, :, :, :]
    nu_mid = visc_part[..., 1:-1, 1:-1]
    nu_east = 0.5 * (nu_mid + visc_part[..., 2:, 1:-1])
    nu_west = 0.5 * (nu_mid + visc_part[..., :-2, 1:-1])
    nu_north = 0.5 * (nu_mid + visc_part[..., 1:-1, 2:])
    nu_south = 0.5 * (nu_mid + visc_part[..., 1:-1, :-2])
    advect = (u_flow * (q_east - q_west) + v_flow * (q_north - q_south)) / (2.0 * spacing)
    diffuse = (
        nu_east * (q_east - centre)
        - nu_west * (centre - q_west)
        + nu_north * (q_north - centre)
        - nu_south * (centre - q_south)
    ) / (spacing * spacing)
    q_above = jnp.concatenate([centre[..., 1:, :, :], centre[..., -1:, :, :]], axis=-3)
    q_below = jnp.concatenate([centre[..., :1, :, :], centre[..., :-1, :, :]], axis=-3)
    return diffuse - advect + vertical_mix * (q_above - 2.0 * centre + q_below)


def coarsen_table(fine_width):
    fine_pos = jnp.arange(fine_width, dtype=jnp.int32)[:, None]
    coarse_pos = jnp.arange(fine_width // 2, dtype=jnp.int32)[None, :]
    weights = (
        0.5 * (fine_pos == 2 * coarse_pos)
        + 0.25 * (fine_pos == 2 * coarse_pos + 1)
        + 0.25 * (fine_pos == 2 * coarse_pos - 1)
        + 0.25 * ((coarse_pos == 0) & (fine_pos == 0))
    )
    return weights.astype(jnp.float32)


def refine_table(coarse_width):
    coarse_pos = jnp.arange(coarse_width, dtype=jnp.int32)[:, None]
    fine_pos = jnp.arange(2 * coarse_width, dtype=jnp.int32)[None, :]
    half_pos = fine_pos // 2
    upper_pos = jnp.minimum(half_pos + 1, coarse_width - 1)
    is_even = fine_pos % 2 == 0
    weights = jnp.where(
        is_even,
        1.0 * (coarse_pos == half_pos),
        0.5 * (coarse_pos == half_pos) + 0.5 * (coarse_pos == upper_pos),
    )
    return weights.astype(jnp.float32)


def on_device(
    fields, viscosity, precursor, tile_index, fine_fields, fine_viscosity, partner_gx, partner_col
):
    highest = lax.Precision.HIGHEST
    nfield, levels, columns, span_cells = fields.shape
    plane_total = precursor.shape[2] * lax.axis_size("gy")
    choose = (tile_index[:, None] == jnp.arange(plane_total, dtype=jnp.int32)[None, :]).astype(
        jnp.float32
    )
    inflow = jnp.einsum(
        "fzp,yp->fzy",
        lax.all_gather(precursor, "gy", axis=2, tiled=True),
        choose,
        precision=highest,
    )
    stacked = jnp.concatenate([fields, viscosity[None]], axis=0)
    padded = padded_2(stacked, (("gx", 2), ("gy", 3)), 1)
    at_inlet = lax.axis_index("gx") == 0
    at_outlet = lax.axis_index("gx") == lax.axis_size("gx") - 1
    inlet_ghost = jnp.concatenate([inflow, viscosity[None, :, 0, :]], axis=0)
    padded = padded.at[:, :, 0, 1:-1].set(jnp.where(at_inlet, inlet_ghost, padded[:, :, 0, 1:-1]))
    padded = padded.at[:, :, -1, 1:-1].set(
        jnp.where(at_outlet, stacked[:, :, -1, :], padded[:, :, -1, 1:-1])
    )
    coarse_rate = tendency(padded, 1.0)
    fine_stack = jnp.concatenate([fine_fields, fine_viscosity[:, None]], axis=1)
    fine_rate = tendency(
        jnp.pad(fine_stack, ((0, 0), (0, 0), (0, 0), (1, 1), (1, 1)), mode="edge"), 0.5
    )
    groups = lax.axis_size("gx")
    slot_count = groups * CAP
    target_hot = (partner_gx[:, None] == jnp.arange(groups, dtype=jnp.int32)[None, :]).astype(
        jnp.int32
    )
    before = jnp.cumsum(target_hot, axis=0) - target_hot
    rank_within = jnp.sum(before * target_hot, axis=1)
    slot_index = partner_gx * CAP + rank_within
    packing = (slot_index[:, None] == jnp.arange(slot_count, dtype=jnp.int32)[None, :]).astype(
        jnp.float32
    )
    col_hot = (partner_col[:, None] == jnp.arange(columns, dtype=jnp.int32)[None, :]).astype(
        jnp.float32
    )
    fine_trace = fine_fields[:, :, :, 0, :]
    to_coarse = coarsen_table(fine_trace.shape[-1])
    to_fine = refine_table(span_cells)
    sending = jnp.einsum("ts,tfzk->sfzk", packing, fine_trace, precision=highest)
    sending = sending.reshape((groups, CAP) + fine_trace.shape[1:])
    columns_out = jnp.einsum("ts,tc->sc", packing, col_hot, precision=highest).reshape(
        groups, CAP, columns
    )
    trace_in = lax.all_to_all(sending, "gx", split_axis=0, concat_axis=0, tiled=True)
    column_in = lax.all_to_all(columns_out, "gx", split_axis=0, concat_axis=0, tiled=True)
    coarse_in = jnp.einsum("gsfzw,wk->gsfzk", trace_in, to_coarse, precision=highest)
    matched = jnp.einsum("gsx,fzxy->gsfzy", column_in, fields, precision=highest)
    answer = jnp.einsum("gsfzk,kw->gsfzw", matched, to_fine, precision=highest)
    returned = lax.all_to_all(answer, "gx", split_axis=0, concat_axis=0, tiled=True)
    mismatch, column_in, returned = (coarse_in - matched, column_in, returned)
    coarse_sat = coarse_penalty * jnp.einsum(
        "gsx,gsfzy->fzxy", column_in, mismatch, precision=highest
    )
    fields_out = fields + time_step * (coarse_rate + coarse_sat)
    coming_back = jnp.einsum(
        "ts,sfzw->tfzw",
        packing,
        returned.reshape((slot_count,) + returned.shape[2:]),
        precision=highest,
    )
    fine_sat = fine_penalty * (coming_back - fine_trace)
    total_rate = fine_rate.at[:, :, :, 0, :].add(fine_sat)
    fine_out = fine_fields + time_step * total_rate
    return (fields_out, fine_out)


def solution(mesh):
    return jax.shard_map(
        on_device,
        mesh=mesh,
        in_specs=(
            P(None, None, "gx", "gy"),
            P(None, "gx", "gy"),
            P(None, None, "gy"),
            P("gy"),
            P(("gx", "gy"), None, None, None, None),
            P(("gx", "gy"), None, None, None),
            P(("gx", "gy")),
            P(("gx", "gy")),
        ),
        out_specs=(P(None, None, "gx", "gy"), P(("gx", "gy"), None, None, None, None)),
        check_vma=False,
    )
```

profile of v0, /device:TPU:58, one launch (start us, length us, event | category | flops | bytes accessed | tf_op | source)
XLA Modules:
  0.0 180.7 jit_solution(5967769567230981480)
XLA Ops:
  0.6 0.7 fusion.91
  1.4 0.8 select_reduce_fusion
  2.2 0.7 multiply_add_fusion.2
  2.9 1.6 fusion.89
  4.5 16.3 %all-to-all-start.1 = ((f32[32,2,32]{2,1,0:T(2,128)}), f32[32,2,32]{2,1,0:T(2,128)S(1)}, u32[]{:S(2)}, u32[]{:S(2)}) async-start(f32[32,2,32]{2,1,0:T(2,128)} %bitcast.19), calls=%async_computation.1 | async-start | bytes 65536 | tf_op jit(solution)/shard_map/all_to_all | solution.py:135
  20.7 2.1 %copy.142 = f32[16,5,4,4,256]{4,0,2,1,3:T(8,128)S(1)} copy(f32[16,5,4,4,256]{4,3,2,1,0:T(4,128)} %param.18) | data formatting | bytes 2621440 | tf_op args[4]
  22.8 0.8 fusion.31
  23.6 1.9 %copy.143 = f32[32,2,5,4,256]{4,3,2,1,0:T(4,128)} copy(f32[32,2,5,4,256]{4,0,3,2,1:T(8,128)S(1)} %fusion.31) | data formatting | bytes 2621440 | tf_op jit(solution)/shard_map/ts,tfzk->sfzk/dot_general | solution.py:129
  25.5 6.8 %all-to-all-done.1 = f32[32,2,32]{2,1,0:T(2,128)S(1)} async-done(((f32[32,2,32]{2,1,0:T(2,128)}), f32[32,2,32]{2,1,0:T(2,128)S(1)}, u32[]{:S(2)}, u32[]{:S(2)}) %all-to-all-start.1) | async-done | bytes 8224 | tf_op jit(solution)/shard_map/all_to_all | solution.py:135
  32.3 6.5 %all-to-all-start = ((f32[32,2,5,4,256]{4,3,2,1,0:T(4,128)}), f32[32,2,5,4,256]{4,3,2,1,0:T(4,128)}, u32[]{:S(2)}, u32[]{:S(2)}) async-start(f32[32,2,5,4,256]{4,3,2,1,0:T(4,128)} %copy.143), calls=%async_computation | async-start | bytes 2621440 | tf_op jit(solution)/shard_map/all_to_all | solution.py:134
  38.8 3.4 %collective-permute-start = (f32[6,4,1,128]{3,2,1,0:T(1,128)S(1)}, f32[6,4,1,128]{3,2,1,0:T(1,128)S(1)}, u32[]{:S(2)}, u32[]{:S(2)}) collective-permute-start(f32[6,4,1,128]{3,2,1,0:T(1,128)S(1)} %get-tuple-element.74), channel_id=1, source_target_pairs={{0,16},{16,32},{32,48},{48,64},{64,80},{80,96},{96,112},{112,128},... | collective-permute-start | bytes 36872 | tf_op jit(solution)/shard_map/ppermute | solution.py:20
  42.2 2.5 %collective-permute-start.1 = (f32[6,4,1,128]{3,2,1,0:T(1,128)S(1)}, f32[6,4,1,128]{3,2,1,0:T(1,128)S(1)}, u32[]{:S(2)}, u32[]{:S(2)}) collective-permute-start(f32[6,4,1,128]{3,2,1,0:T(1,128)S(1)} %get-tuple-element.75), channel_id=1, source_target_pairs={{16,0},{32,16},{48,32},{64,48},{80,64},{96,80},{112,96},{128,112},... | collective-permute-start | bytes 36872 | tf_op jit(solution)/shard_map/ppermute | solution.py:22
  44.9 1.1 slice_bitcast_fusion.1
  46.0 0.2 copy.156
  46.4 24.0 %all_gather.3 = f32[5,4,512]{0,1,2:T(4,128)} all-gather(f32[5,4,32]{0,1,2:T(4,128)S(1)} %copy.138), channel_id=1, replica_groups=mesh['gx'=32,'gy'=16] {'gy'}, dimensions={2}, use_global_device_ids=true | all-gather | bytes 43520 | tf_op jit(solution)/shard_map/all_gather | solution.py:94
  70.4 1.6 copy.167
  72.0 0.6 fusion.110
  72.7 0.7 fusion.29
  73.4 1.2 fusion.49
  74.6 1.9 %copy.163 = f32[32,2,5,4,256]{4,3,2,1,0:T(4,128)} copy(f32[32,2,5,4,256]{4,0,3,2,1:T(8,128)S(1)} %fusion.49) | data formatting | bytes 2621440 | tf_op jit(solution)/shard_map/gsfzk,kw->gsfzw/dot_general | solution.py:138
  76.5 27.4 %all-to-all-done = f32[32,2,5,4,256]{4,3,2,1,0:T(4,128)} async-done(((f32[32,2,5,4,256]{4,3,2,1,0:T(4,128)}), f32[32,2,5,4,256]{4,3,2,1,0:T(4,128)}, u32[]{:S(2)}, u32[]{:S(2)}) %all-to-all-start) | async-done | bytes 1310752 | tf_op jit(solution)/shard_map/all_to_all | solution.py:134
  103.9 4.6 %all-to-all-start.2 = ((f32[32,2,5,4,256]{4,3,2,1,0:T(4,128)}), f32[32,2,5,4,256]{4,3,2,1,0:T(4,128)}, u32[]{:S(2)}, u32[]{:S(2)}) async-start(f32[32,2,5,4,256]{4,3,2,1,0:T(4,128)} %copy.163), calls=%async_computation.2 | async-start | bytes 2621440 | tf_op jit(solution)/shard_map/all_to_all | solution.py:139
  108.6 0.2 pad_maximum_fusion
  108.9 0.4 copy-done.5
  109.3 0.3 fusion.43
  109.6 0.4 fusion.104
  110.1 0.2 fusion.37
  110.3 0.3 fusion.106
  110.6 3.0 %fusion.2 = f32[16,5,4,4,256]{4,0,2,1,3:T(8,128)} fusion(f32[16,5,1,4,256]{4,0,2,1,3:T(8,128)S(1)} %get-tuple-element.59, f32[16,5,3,4,256]{4,0,2,1,3:T(8,128)S(1)} %get-tuple-element.61, f32[16,5,3,4,256]{4,0,2,1,3:T(8,128)S(1)} %get-tuple-element.60, f32[16,5,1,4,256]{4,0,2,1,3:T(8,128)S(1)} %get-tuple-element.58, f32[16,5,4,4,256]{4,0,2,1,3:T(8,128)S(1)} %copy.142, ...), kind=kLoop, calls=%fused_computation.16 | loop fusion | flops 12124160 | bytes 7882752 | tf_op jit(solution)/shard_map/add | solution.py:54
  113.7 0.2 fusion.109
  113.9 0.3 copy.134
  114.1 1.9 %collective-permute-start.2 = (f32[6,4,34,1]{2,1,3,0:T(4,128)S(1)}, f32[6,4,34,1]{2,1,3,0:T(4,128)S(1)}, u32[]{:S(2)}, u32[]{:S(2)}) collective-permute-start(f32[6,4,34,1]{2,1,3,0:T(4,128)S(1)} %copy.134), channel_id=1, source_target_pairs={{0,1},{1,2},{2,3},{3,4},{4,5},{5,6},{6,7},{7,8},{8,9},{9,10},{10,1... | collective-permute-start | bytes 9800 | tf_op jit(solution)/shard_map/ppermute | solution.py:20
  116.0 0.3 copy.135
  116.3 3.8 %collective-permute-start.3 = (f32[6,4,34,1]{2,1,3,0:T(4,128)S(1)}, f32[6,4,34,1]{2,1,3,0:T(4,128)S(1)}, u32[]{:S(2)}, u32[]{:S(2)}) collective-permute-start(f32[6,4,34,1]{2,1,3,0:T(4,128)S(1)} %copy.135), channel_id=1, source_target_pairs={{1,0},{2,1},{3,2},{4,3},{5,4},{6,5},{7,6},{8,7},{9,8},{10,9},{11,1... | collective-permute-start | bytes 9800 | tf_op jit(solution)/shard_map/ppermute | solution.py:22
  120.2 1.1 copy.136
  121.3 1.1 copy.137
  122.4 1.7 pad_maximum_fusion.13
  124.1 5.1 %scatter.6 = f32[6,4,34,130]{3,2,1,0:T(8,128)S(1)} dynamic-update-slice(f32[6,4,34,130]{3,2,1,0:T(8,128)S(1)} %pad_maximum_fusion.13, f32[6,4,1,128]{3,2,1,0:T(1,128)S(1)} %broadcast_select_fusion.1, s32[]{:T(128)} %constant.156.clone.1, s32[]{:T(128)} %constant.156.clone.1, s32[]{:T(128)} %bitcast.5, s32[]{:T(128)} %bitcast.6) | dynamic-update-slice | bytes 24580 | tf_op jit(solution)/shard_map/scatter | solution.py:103
  129.3 3.8 %scatter.9 = f32[6,4,34,130]{3,2,1,0:T(8,128)S(1)} dynamic-update-slice(f32[6,4,34,130]{3,2,1,0:T(8,128)S(1)} %scatter.6, f32[6,4,1,128]{3,2,1,0:T(1,128)S(1)} %broadcast_select_fusion, s32[]{:T(128)} %constant.156.clone.1, s32[]{:T(128)} %constant.156.clone.1, s32[]{:T(128)} %constant.158.clone.1, s32[]{:T(128)} %constant.159.clone.1) | dynamic-update-slice | bytes 24580 | tf_op jit(solution)/shard_map/scatter | solution.py:104
  133.2 0.2 fusion.71
  133.4 0.2 fusion.108
  133.6 2.8 %fusion.7 = f32[32,2,5,4,128]{4,0,3,2,1:T(8,128)S(1)} fusion(f32[32,2,5,4,128]{4,0,3,2,1:T(8,128)S(1)} %fusion.29, f32[32,2,5,4,256]{4,3,2,1,0:T(4,128)} %all-to-all-done, s32[128]{0:T(128)S(1)} %get-tuple-element.79, s32[128]{0:T(128)S(1)} %broadcast_add_fusion.1, s32[128]{0:T(128)S(1)} %get-tuple-element.78, pred[128]{0:T(512)(128)(4,1)S(1)} %iota_compare_fusion.16, ...), kind=kOutput, calls=%fused_computation.22 | convolution fusion | flops 503840768 | bytes 2623360 | tf_op jit(solution)/shard_map/gsfzw,wk->gsfzk/dot_general | solution.py:136
  136.4 0.5 convolution_bitcast_fusion
  136.9 1.2 fusion.28
  138.1 35.8 %all-to-all-done.2 = f32[32,2,5,4,256]{4,3,2,1,0:T(4,128)} async-done(((f32[32,2,5,4,256]{4,3,2,1,0:T(4,128)}), f32[32,2,5,4,256]{4,3,2,1,0:T(4,128)}, u32[]{:S(2)}, u32[]{:S(2)}) %all-to-all-start.2) | async-done | bytes 1310752 | tf_op jit(solution)/shard_map/all_to_all | solution.py:139
  173.9 2.7 %fusion.19 = f32[16,5,4,4,256]{4,0,2,1,3:T(8,128)} fusion(f32[16,5,4,4,256]{4,0,2,1,3:T(8,128)} %fusion.2, f32[64,5,4,256]{3,2,1,0:T(4,128)} %bitcast.36, f32[16,5,4,4,256]{4,0,2,1,3:T(8,128)S(1)} %copy.142, s32[16]{0:T(128)S(1)} %multiply_add_fusion.2), kind=kOutput, calls=%fused_computation.27 | convolution fusion | flops 63079424 | bytes 2293824 | tf_op jit(solution)/shard_map/ts,sfzw->tfzw/dot_general | solution.py:145
  176.6 2.2 %multiply_add_fusion = f32[16,5,4,4,256]{4,0,2,1,3:T(8,128)S(1)} fusion(f32[16,5,4,4,256]{4,0,2,1,3:T(8,128)} %fusion.19, f32[16,5,4,4,256]{4,3,2,1,0:T(4,128)S(1)} %copy-done.1), kind=kLoop, calls=%fused_computation.21 | loop fusion | flops 655360 | bytes 3932160 | tf_op jit(solution)/shard_map/add | solution.py:153
  178.8 1.9 %copy.166 = f32[16,5,4,4,256]{4,3,2,1,0:T(4,128)} copy(f32[16,5,4,4,256]{4,0,2,1,3:T(8,128)S(1)} %multiply_add_fusion) | data formatting | bytes 2621440
  (36 shorter events, 1.1 us)
Async XLA Ops:
  4.5 27.9 %all-to-all-start.1 = ((f32[32,2,32]{2,1,0:T(2,128)}), f32[32,2,32]{2,1,0:T(2,128)S(1)}, u32[]{:S(2)}, u32[]{:S(2)}) async-start(f32[32,2,32]{2,1,0:T(2,128)} %bitcast.19), calls=%async_computation.1 | async-start | bytes 65536 | tf_op jit(solution)/shard_map/all_to_all | solution.py:135
  25.5 13.3 %copy-start = (f32[5,4,32,128]{3,2,1,0:T(8,128)S(1)}, f32[5,4,32,128]{3,2,1,0:T(8,128)}, u32[]{:S(2)}) copy-start(f32[5,4,32,128]{3,2,1,0:T(8,128)} %param.14) | copy-start | bytes 983044
  25.5 13.3 %copy-start.2 = (f32[4,32,128]{2,1,0:T(8,128)S(1)}, f32[4,32,128]{2,1,0:T(8,128)}, u32[]{:S(2)}) copy-start(f32[4,32,128]{2,1,0:T(8,128)} %param.15) | copy-start | bytes 196612
  25.5 19.2 %copy-start.3 = (f32[16,4,4,256]{3,2,1,0:T(4,128)S(1)}, f32[16,4,4,256]{3,2,1,0:T(4,128)}, u32[]{:S(2)}) copy-start(f32[16,4,4,256]{3,2,1,0:T(4,128)} %param.19) | copy-start | bytes 786436
  32.3 71.6 %all-to-all-start = ((f32[32,2,5,4,256]{4,3,2,1,0:T(4,128)}), f32[32,2,5,4,256]{4,3,2,1,0:T(4,128)}, u32[]{:S(2)}, u32[]{:S(2)}) async-start(f32[32,2,5,4,256]{4,3,2,1,0:T(4,128)} %copy.143), calls=%async_computation | async-start | bytes 2621440 | tf_op jit(solution)/shard_map/all_to_all | solution.py:134
  38.8 74.8 %collective-permute-start = (f32[6,4,1,128]{3,2,1,0:T(1,128)S(1)}, f32[6,4,1,128]{3,2,1,0:T(1,128)S(1)}, u32[]{:S(2)}, u32[]{:S(2)}) collective-permute-start(f32[6,4,1,128]{3,2,1,0:T(1,128)S(1)} %get-tuple-element.74), channel_id=1, source_target_pairs={{0,16},{16,32},{32,48},{48,64},{64,80},{80,96},{96,112},{112,128},... | collective-permute-start | bytes 36872 | tf_op jit(solution)/shard_map/ppermute | solution.py:20
  42.2 4.1 %copy-start.4 = (f32[5,4,32]{2,1,0:T(4,128)S(1)}, f32[5,4,32]{2,1,0:T(4,128)}, u32[]{:S(2)}) copy-start(f32[5,4,32]{2,1,0:T(4,128)} %param.16) | copy-start | bytes 7684
  42.2 71.4 %collective-permute-start.1 = (f32[6,4,1,128]{3,2,1,0:T(1,128)S(1)}, f32[6,4,1,128]{3,2,1,0:T(1,128)S(1)}, u32[]{:S(2)}, u32[]{:S(2)}) collective-permute-start(f32[6,4,1,128]{3,2,1,0:T(1,128)S(1)} %get-tuple-element.75), channel_id=1, source_target_pairs={{16,0},{32,16},{48,32},{64,48},{80,64},{96,80},{112,96},{128,112},... | collective-permute-start | bytes 36872 | tf_op jit(solution)/shard_map/ppermute | solution.py:22
  103.9 70.0 %all-to-all-start.2 = ((f32[32,2,5,4,256]{4,3,2,1,0:T(4,128)}), f32[32,2,5,4,256]{4,3,2,1,0:T(4,128)}, u32[]{:S(2)}, u32[]{:S(2)}) async-start(f32[32,2,5,4,256]{4,3,2,1,0:T(4,128)} %copy.163), calls=%async_computation.2 | async-start | bytes 2621440 | tf_op jit(solution)/shard_map/all_to_all | solution.py:139
  108.6 0.7 copy-start.5
  114.1 6.0 %collective-permute-start.2 = (f32[6,4,34,1]{2,1,3,0:T(4,128)S(1)}, f32[6,4,34,1]{2,1,3,0:T(4,128)S(1)}, u32[]{:S(2)}, u32[]{:S(2)}) collective-permute-start(f32[6,4,34,1]{2,1,3,0:T(4,128)S(1)} %copy.134), channel_id=1, source_target_pairs={{0,1},{1,2},{2,3},{3,4},{4,5},{5,6},{6,7},{7,8},{8,9},{9,10},{10,1... | collective-permute-start | bytes 9800 | tf_op jit(solution)/shard_map/ppermute | solution.py:20
  116.3 5.0 %collective-permute-start.3 = (f32[6,4,34,1]{2,1,3,0:T(4,128)S(1)}, f32[6,4,34,1]{2,1,3,0:T(4,128)S(1)}, u32[]{:S(2)}, u32[]{:S(2)}) collective-permute-start(f32[6,4,34,1]{2,1,3,0:T(4,128)S(1)} %copy.135), channel_id=1, source_target_pairs={{1,0},{2,1},{3,2},{4,3},{5,4},{6,5},{7,6},{8,7},{9,8},{10,9},{11,1... | collective-permute-start | bytes 9800 | tf_op jit(solution)/shard_map/ppermute | solution.py:22
  138.1 38.5 %copy-start.1 = (f32[16,5,4,4,256]{4,3,2,1,0:T(4,128)S(1)}, f32[16,5,4,4,256]{4,3,2,1,0:T(4,128)}, u32[]{:S(2)}) copy-start(f32[16,5,4,4,256]{4,3,2,1,0:T(4,128)} %param.18) | copy-start | bytes 3932164
where the time goes:
time: 181 us
  waiting for transfers between devices  70.1 us (39%)
  starting transfers between devices  38.9 us (21%)
  local copies, waits for them, and re-layouts  24.8 us (14%)
  blocking collectives  24 us (13%)
  other arithmetic  11.4 us (6%)
  matrix products  10.6 us (6%)
    all_to_all x1, waiting for transfers between devices, on_device(): lax.all_to_all(answer, 'gx', split_axis=0, concat_axis=0, tiled=True)  35.8 us
    all_to_all x1, waiting for transfers between devices, on_device(): lax.all_to_all(sending, 'gx', split_axis=0, concat_axis=0, tiled=True)  27.4 us
    all_gather x1, blocking collectives, on_device(): lax.all_gather(precursor, 'gy', axis=2, tiled=True)  24 us
    all_to_all x1, starting transfers between devices, on_device(): lax.all_to_all(columns_out, 'gx', split_axis=0, concat_axis=0, tiled=True)  16.3 us
    all_to_all x1, waiting for transfers between devices, on_device(): lax.all_to_all(columns_out, 'gx', split_axis=0, concat_axis=0, tiled=True)  6.83 us
    all_to_all x1, starting transfers between devices, on_device(): lax.all_to_all(sending, 'gx', split_axis=0, concat_axis=0, tiled=True)  6.45 us
    ppermute x2, starting transfers between devices, padded_2(): lax.ppermute(head, axis, [((i + 1) % count, i) for i in range(count)])  6.29 us
    ppermute x2, starting transfers between devices, padded_2(): lax.ppermute(tail, axis, [(i, (i + 1) % count) for i in range(count)])  5.29 us
  transfers between devices with their start and end apart: 7, of which 4 were waited for; matrix products, arithmetic and copies ran while one was open for 20% of the time, Pallas kernels for 0%

commit v1 on v0

--- a/solution.py
+++ b/solution.py
@@ -91,7 +91,9 @@
     )
     inflow = jnp.einsum(
         "fzp,yp->fzy",
-        lax.all_gather(precursor, "gy", axis=2, tiled=True),
+        jnp.concatenate(
+            lax.all_to_all(jnp.stack([precursor] * lax.axis_size("gy")), "gy", 0, 0), axis=2
+        ),
         choose,
         precision=highest,
     )

time: 181 us -> 197 us (1.088)
  the two profiles are of different devices: /device:TPU:58 before, /device:TPU:40 now
where the time goes in v1:
time: 197 us; the launch traced here: 196 us
  waiting for transfers between devices  87.9 us (45%)
  starting transfers between devices  49.9 us (25%)
  local copies, waits for them, and re-layouts  28.8 us (15%)
  other arithmetic  16.7 us (8%)
  matrix products  11.9 us (6%)
    all_to_all x1, waiting for transfers between devices, on_device(): lax.all_to_all(sending, 'gx', split_axis=0, concat_axis=0, tiled=True)  49.1 us
    all_to_all x1, waiting for transfers between devices, on_device(): lax.all_to_all(answer, 'gx', split_axis=0, concat_axis=0, tiled=True)  25.2 us
    all_to_all x1, starting transfers between devices, on_device(): lax.all_to_all(columns_out, 'gx', split_axis=0, concat_axis=0, tiled=True)  16.3 us
    ppermute x2, starting transfers between devices, padded_2(): lax.ppermute(head, axis, [((i + 1) % count, i) for i in range(count)])  9.89 us
    all_to_all x1, waiting for transfers between devices, on_device(): lax.all_to_all(columns_out, 'gx', split_axis=0, concat_axis=0, tiled=True)  8.7 us
    all_to_all x1, starting transfers between devices, on_device(): lax.all_to_all(sending, 'gx', split_axis=0, concat_axis=0, tiled=True)  6.9 us
    all_to_all x1, starting transfers between devices, on_device(): lax.all_to_all(jnp.stack([precursor] * lax.axis_size('gy')), 'gy', 0, 0)  6.14 us
    unnamed x37, local copies, waits for them, and re-layouts  5.85 us
  transfers between devices with their start and end apart: 8, of which 4 were waited for; matrix products, arithmetic and copies ran while one was open for 23% of the time, Pallas kernels for 0%

profile of v1, /device:TPU:40, one launch (start us, length us, event | category | flops | bytes accessed | tf_op | source)
XLA Modules:
  0.0 196.2 jit_solution(12936528930870753441)
XLA Ops:
  0.6 0.7 fusion.91
  1.4 0.8 select_reduce_fusion
  2.2 0.7 multiply_add_fusion.2
  2.9 1.6 fusion.89
  4.5 16.3 %all-to-all-start.2 = ((f32[32,2,32]{2,1,0:T(2,128)}), f32[32,2,32]{2,1,0:T(2,128)S(1)}, u32[]{:S(2)}, u32[]{:S(2)}) async-start(f32[32,2,32]{2,1,0:T(2,128)} %bitcast.20), calls=%async_computation.2 | async-start | bytes 65536 | tf_op jit(solution)/shard_map/all_to_all | solution.py:137
  20.7 2.1 %copy.142 = f32[16,5,4,4,256]{4,0,2,1,3:T(8,128)S(1)} copy(f32[16,5,4,4,256]{4,3,2,1,0:T(4,128)} %param.18) | data formatting | bytes 2621440 | tf_op args[4]
  22.9 0.8 reshape.265
  23.6 8.7 %all-to-all-done.2 = f32[32,2,32]{2,1,0:T(2,128)S(1)} async-done(((f32[32,2,32]{2,1,0:T(2,128)}), f32[32,2,32]{2,1,0:T(2,128)S(1)}, u32[]{:S(2)}, u32[]{:S(2)}) %all-to-all-start.2) | async-done | bytes 8224 | tf_op jit(solution)/shard_map/all_to_all | solution.py:137
  32.3 6.1 %all-to-all-start = ((f32[16,1,640]{2,1,0:T(1,128)}), f32[16,1,640]{2,1,0:T(1,128)S(1)}, u32[]{:S(2)}, u32[]{:S(2)}) async-start(f32[16,1,640]{2,1,0:T(1,128)} %reshape.265), calls=%async_computation | async-start | bytes 81920 | tf_op jit(solution)/shard_map/all_to_all | solution.py:95
  38.5 0.8 fusion.31
  39.3 1.9 copy.143
  41.2 4.9 %all-to-all-done = f32[16,1,640]{2,1,0:T(1,128)S(1)} async-done(((f32[16,1,640]{2,1,0:T(1,128)}), f32[16,1,640]{2,1,0:T(1,128)S(1)}, u32[]{:S(2)}, u32[]{:S(2)}) %all-to-all-start) | async-done | bytes 40992 | tf_op jit(solution)/shard_map/all_to_all | solution.py:95
  46.1 6.9 %all-to-all-start.1 = ((f32[32,2,5,4,256]{4,3,2,1,0:T(4,128)}), f32[32,2,5,4,256]{4,3,2,1,0:T(4,128)}, u32[]{:S(2)}, u32[]{:S(2)}) async-start(f32[32,2,5,4,256]{4,3,2,1,0:T(4,128)} %copy.143), calls=%async_computation.1 | async-start | bytes 2621440 | tf_op jit(solution)/shard_map/all_to_all | solution.py:136
  53.0 0.6 pad_maximum_fusion.18
  53.6 3.4 %collective-permute-start = (f32[6,4,1,128]{3,2,1,0:T(1,128)S(1)}, f32[6,4,1,128]{3,2,1,0:T(1,128)S(1)}, u32[]{:S(2)}, u32[]{:S(2)}) collective-permute-start(f32[6,4,1,128]{3,2,1,0:T(1,128)S(1)} %get-tuple-element.74), channel_id=1, source_target_pairs={{0,16},{16,32},{32,48},{48,64},{64,80},{80,96},{96,112},{112,128},... | collective-permute-start | bytes 36872 | tf_op jit(solution)/shard_map/ppermute | solution.py:20
  57.0 2.5 %collective-permute-start.1 = (f32[6,4,1,128]{3,2,1,0:T(1,128)}, f32[6,4,1,128]{3,2,1,0:T(1,128)S(1)}, u32[]{:S(2)}, u32[]{:S(2)}) collective-permute-start(f32[6,4,1,128]{3,2,1,0:T(1,128)} %get-tuple-element.75), channel_id=1, source_target_pairs={{16,0},{32,16},{48,32},{64,48},{80,64},{96,80},{112,96},{128,112},... | collective-permute-start | bytes 36872 | tf_op jit(solution)/shard_map/ppermute | solution.py:22
  59.7 1.1 slice_bitcast_fusion.1
  60.7 0.9 copy.156
  61.6 0.9 copy.157
  64.1 0.7 fusion.110
  64.9 0.7 fusion.29
  65.6 1.8 fusion.49
  67.5 1.9 copy.163
  69.4 49.1 %all-to-all-done.1 = f32[32,2,5,4,256]{4,3,2,1,0:T(4,128)} async-done(((f32[32,2,5,4,256]{4,3,2,1,0:T(4,128)}), f32[32,2,5,4,256]{4,3,2,1,0:T(4,128)}, u32[]{:S(2)}, u32[]{:S(2)}) %all-to-all-start.1) | async-done | bytes 1310752 | tf_op jit(solution)/shard_map/all_to_all | solution.py:136
  118.5 5.5 %all-to-all-start.3 = ((f32[32,2,5,4,256]{4,3,2,1,0:T(4,128)}), f32[32,2,5,4,256]{4,3,2,1,0:T(4,128)}, u32[]{:S(2)}, u32[]{:S(2)}) async-start(f32[32,2,5,4,256]{4,3,2,1,0:T(4,128)} %copy.163), calls=%async_computation.3 | async-start | bytes 2621440 | tf_op jit(solution)/shard_map/all_to_all | solution.py:141
  124.0 0.6 broadcast_add_fusion.1
  124.8 0.6 slice_bitcast_fusion.4
  126.4 0.7 copy-done.2
  127.2 3.0 %fusion.2 = f32[16,5,4,4,256]{4,0,2,1,3:T(8,128)} fusion(f32[16,5,1,4,256]{4,0,2,1,3:T(8,128)S(1)} %get-tuple-element.59, f32[16,5,3,4,256]{4,0,2,1,3:T(8,128)S(1)} %get-tuple-element.61, f32[16,5,3,4,256]{4,0,2,1,3:T(8,128)S(1)} %get-tuple-element.60, f32[16,5,1,4,256]{4,0,2,1,3:T(8,128)S(1)} %get-tuple-element.58, f32[16,5,4,4,256]{4,0,2,1,3:T(8,128)S(1)} %copy.142, ...), kind=kLoop, calls=%fused_computation.16 | loop fusion | flops 12124160 | bytes 7882752 | tf_op jit(solution)/shard_map/add | solution.py:54
  131.2 1.9 collective-permute-start.2
  133.4 7.4 %collective-permute-start.3 = (f32[6,4,34,1]{2,1,3,0:T(4,128)S(1)}, f32[6,4,34,1]{2,1,3,0:T(4,128)S(1)}, u32[]{:S(2)}, u32[]{:S(2)}) collective-permute-start(f32[6,4,34,1]{2,1,3,0:T(4,128)S(1)} %copy.135), channel_id=1, source_target_pairs={{1,0},{2,1},{3,2},{4,3},{5,4},{6,5},{7,6},{8,7},{9,8},{10,9},{11,1... | collective-permute-start | bytes 9800 | tf_op jit(solution)/shard_map/ppermute | solution.py:22
  140.8 0.6 iota_compare_fusion.16
  141.4 1.1 copy.136
  142.5 1.1 copy.137
  143.6 1.7 pad_maximum_fusion.13
  145.8 0.7 reduce.6
  146.7 0.7 copy.138
  147.4 1.0 reshape.264
  148.4 1.0 fusion.43
  149.4 0.7 broadcast_select_fusion.1
  150.2 5.0 %scatter.6 = f32[6,4,34,130]{3,2,1,0:T(8,128)S(1)} dynamic-update-slice(f32[6,4,34,130]{3,2,1,0:T(8,128)S(1)} %pad_maximum_fusion.13, f32[6,4,1,128]{3,2,1,0:T(1,128)S(1)} %broadcast_select_fusion.1, s32[]{:T(128)} %constant.156.clone.1, s32[]{:T(128)} %constant.156.clone.1, s32[]{:T(128)} %bitcast.6, s32[]{:T(128)} %bitcast.7) | dynamic-update-slice | bytes 24580 | tf_op jit(solution)/shard_map/scatter | solution.py:105
  155.3 3.8 %scatter.9 = f32[6,4,34,130]{3,2,1,0:T(8,128)S(1)} dynamic-update-slice(f32[6,4,34,130]{3,2,1,0:T(8,128)S(1)} %scatter.6, f32[6,4,1,128]{3,2,1,0:T(1,128)S(1)} %broadcast_select_fusion, s32[]{:T(128)} %constant.156.clone.1, s32[]{:T(128)} %constant.156.clone.1, s32[]{:T(128)} %constant.158.clone.1, s32[]{:T(128)} %constant.159.clone.1) | dynamic-update-slice | bytes 24580 | tf_op jit(solution)/shard_map/scatter | solution.py:106
  159.7 2.8 %fusion.7 = f32[32,2,5,4,128]{4,0,3,2,1:T(8,128)S(1)} fusion(f32[32,2,5,4,128]{4,0,3,2,1:T(8,128)S(1)} %fusion.29, f32[32,2,5,4,256]{4,3,2,1,0:T(4,128)} %all-to-all-done.1, s32[128]{0:T(128)S(1)} %copy-done.12, s32[128]{0:T(128)S(1)} %copy-done.13, s32[128]{0:T(128)S(1)} %copy-done.11, pred[128]{0:T(512)(128)(4,1)S(1)} %copy-done.15, ...), kind=kOutput, calls=%fused_computation.22 | convolution fusion | flops 503840768 | bytes 2623360 | tf_op jit(solution)/shard_map/gsfzw,wk->gsfzk/dot_general | solution.py:138
  163.0 1.2 fusion.28
  164.2 25.2 %all-to-all-done.3 = f32[32,2,5,4,256]{4,3,2,1,0:T(4,128)} async-done(((f32[32,2,5,4,256]{4,3,2,1,0:T(4,128)}), f32[32,2,5,4,256]{4,3,2,1,0:T(4,128)}, u32[]{:S(2)}, u32[]{:S(2)}) %all-to-all-start.3) | async-done | bytes 1310752 | tf_op jit(solution)/shard_map/all_to_all | solution.py:141
  189.4 2.7 %fusion.19 = f32[16,5,4,4,256]{4,0,2,1,3:T(8,128)} fusion(f32[16,5,4,4,256]{4,0,2,1,3:T(8,128)} %fusion.2, f32[64,5,4,256]{3,2,1,0:T(4,128)} %bitcast.37, f32[16,5,4,4,256]{4,0,2,1,3:T(8,128)S(1)} %copy.142, s32[16]{0:T(128)S(1)} %copy-done.10), kind=kOutput, calls=%fused_computation.27 | convolution fusion | flops 63079424 | bytes 2293824 | tf_op jit(solution)/shard_map/ts,sfzw->tfzw/dot_general | solution.py:147
  192.1 2.2 %multiply_add_fusion = f32[16,5,4,4,256]{4,0,2,1,3:T(8,128)S(1)} fusion(f32[16,5,4,4,256]{4,0,2,1,3:T(8,128)} %fusion.19, f32[16,5,4,4,256]{4,3,2,1,0:T(4,128)S(1)} %copy-done.1), kind=kLoop, calls=%fused_computation.21 | loop fusion | flops 655360 | bytes 3932160 | tf_op jit(solution)/shard_map/add | solution.py:155
  194.3 1.9 copy.166
  (62 shorter events, 6.3 us)
Async XLA Ops:
  2.9 35.6 %copy-start.9 = (s32[16]{0:T(128)}, s32[16]{0:T(128)S(1)}, u32[]{:S(2)}) copy-start(s32[16]{0:T(128)S(1)} %multiply_add_fusion.2) | copy-start | bytes 196
  4.5 27.9 %all-to-all-start.2 = ((f32[32,2,32]{2,1,0:T(2,128)}), f32[32,2,32]{2,1,0:T(2,128)S(1)}, u32[]{:S(2)}, u32[]{:S(2)}) async-start(f32[32,2,32]{2,1,0:T(2,128)} %bitcast.20), calls=%async_computation.2 | async-start | bytes 65536 | tf_op jit(solution)/shard_map/all_to_all | solution.py:137
  20.7 2.1 %copy-start.8 = (f32[5,4,32]{2,1,0:T(4,128)S(1)}, f32[5,4,32]{2,1,0:T(4,128)}, u32[]{:S(2)}) copy-start(f32[5,4,32]{2,1,0:T(4,128)} %param.16) | copy-start | bytes 7684
  32.3 13.8 %all-to-all-start = ((f32[16,1,640]{2,1,0:T(1,128)}), f32[16,1,640]{2,1,0:T(1,128)S(1)}, u32[]{:S(2)}, u32[]{:S(2)}) async-start(f32[16,1,640]{2,1,0:T(1,128)} %reshape.265), calls=%async_computation | async-start | bytes 81920 | tf_op jit(solution)/shard_map/all_to_all | solution.py:95
  41.2 11.8 %copy-start = (f32[5,4,32,128]{3,2,1,0:T(8,128)S(1)}, f32[5,4,32,128]{3,2,1,0:T(8,128)}, u32[]{:S(2)}) copy-start(f32[5,4,32,128]{3,2,1,0:T(8,128)} %param.14) | copy-start | bytes 983044
  41.2 11.8 %copy-start.4 = (f32[4,32,128]{2,1,0:T(8,128)S(1)}, f32[4,32,128]{2,1,0:T(8,128)}, u32[]{:S(2)}) copy-start(f32[4,32,128]{2,1,0:T(8,128)} %param.15) | copy-start | bytes 196612
  41.2 18.3 %copy-start.5 = (f32[16,4,4,256]{3,2,1,0:T(4,128)S(1)}, f32[16,4,4,256]{3,2,1,0:T(4,128)}, u32[]{:S(2)}) copy-start(f32[16,4,4,256]{3,2,1,0:T(4,128)} %param.19) | copy-start | bytes 786436
  46.1 72.4 %all-to-all-start.1 = ((f32[32,2,5,4,256]{4,3,2,1,0:T(4,128)}), f32[32,2,5,4,256]{4,3,2,1,0:T(4,128)}, u32[]{:S(2)}, u32[]{:S(2)}) async-start(f32[32,2,5,4,256]{4,3,2,1,0:T(4,128)} %copy.143), calls=%async_computation.1 | async-start | bytes 2621440 | tf_op jit(solution)/shard_map/all_to_all | solution.py:136
  53.6 8.8 %copy-start.7 = (f32[6,4,1,128]{3,2,1,0:T(1,128)}, f32[6,4,1,128]{3,2,1,0:T(1,128)S(1)}, u32[]{:S(2)}) copy-start(f32[6,4,1,128]{3,2,1,0:T(1,128)S(1)} %get-tuple-element.74) | copy-start | bytes 36868
  53.6 77.0 %collective-permute-start = (f32[6,4,1,128]{3,2,1,0:T(1,128)S(1)}, f32[6,4,1,128]{3,2,1,0:T(1,128)S(1)}, u32[]{:S(2)}, u32[]{:S(2)}) collective-permute-start(f32[6,4,1,128]{3,2,1,0:T(1,128)S(1)} %get-tuple-element.74), channel_id=1, source_target_pairs={{0,16},{16,32},{32,48},{48,64},{64,80},{80,96},{96,112},{112,128},... | collective-permute-start | bytes 36872 | tf_op jit(solution)/shard_map/ppermute | solution.py:20
  57.0 73.7 %collective-permute-start.1 = (f32[6,4,1,128]{3,2,1,0:T(1,128)}, f32[6,4,1,128]{3,2,1,0:T(1,128)S(1)}, u32[]{:S(2)}, u32[]{:S(2)}) collective-permute-start(f32[6,4,1,128]{3,2,1,0:T(1,128)} %get-tuple-element.75), channel_id=1, source_target_pairs={{16,0},{32,16},{48,32},{64,48},{80,64},{96,80},{112,96},{128,112},... | collective-permute-start | bytes 36872 | tf_op jit(solution)/shard_map/ppermute | solution.py:22
  118.5 70.9 %all-to-all-start.3 = ((f32[32,2,5,4,256]{4,3,2,1,0:T(4,128)}), f32[32,2,5,4,256]{4,3,2,1,0:T(4,128)}, u32[]{:S(2)}, u32[]{:S(2)}) async-start(f32[32,2,5,4,256]{4,3,2,1,0:T(4,128)} %copy.163), calls=%async_computation.3 | async-start | bytes 2621440 | tf_op jit(solution)/shard_map/all_to_all | solution.py:141
  126.1 1.0 copy-start.2
  126.1 1.0 copy-start.3
  130.7 12.9 %copy-start.6 = (f32[6,4,1,128]{3,2,1,0:T(1,128)}, f32[6,4,1,128]{3,2,1,0:T(1,128)S(1)}, u32[]{:S(2)}) copy-start(f32[6,4,1,128]{3,2,1,0:T(1,128)S(1)} %collective-permute-done) | copy-start | bytes 36868
  131.2 10.2 %collective-permute-start.2 = (f32[6,4,34,1]{2,1,3,0:T(4,128)S(1)}, f32[6,4,34,1]{2,1,3,0:T(4,128)S(1)}, u32[]{:S(2)}, u32[]{:S(2)}) collective-permute-start(f32[6,4,34,1]{2,1,3,0:T(4,128)S(1)} %copy.134), channel_id=1, source_target_pairs={{0,1},{1,2},{2,3},{3,4},{4,5},{5,6},{6,7},{7,8},{8,9},{9,10},{10,1... | collective-permute-start | bytes 9800 | tf_op jit(solution)/shard_map/ppermute | solution.py:20
  133.4 9.1 %collective-permute-start.3 = (f32[6,4,34,1]{2,1,3,0:T(4,128)S(1)}, f32[6,4,34,1]{2,1,3,0:T(4,128)S(1)}, u32[]{:S(2)}, u32[]{:S(2)}) collective-permute-start(f32[6,4,34,1]{2,1,3,0:T(4,128)S(1)} %copy.135), channel_id=1, source_target_pairs={{1,0},{2,1},{3,2},{4,3},{5,4},{6,5},{7,6},{8,7},{9,8},{10,9},{11,1... | collective-permute-start | bytes 9800 | tf_op jit(solution)/shard_map/ppermute | solution.py:22
  147.4 12.2 %copy-start.11 = (s32[128]{0:T(128)S(1)}, s32[128]{0:T(128)}, u32[]{:S(2)}) copy-start(s32[128]{0:T(128)} %get-tuple-element.78) | copy-start | bytes 1540
  147.4 12.2 %copy-start.12 = (s32[128]{0:T(128)S(1)}, s32[128]{0:T(128)}, u32[]{:S(2)}) copy-start(s32[128]{0:T(128)} %get-tuple-element.79) | copy-start | bytes 1540
  147.4 12.3 %copy-start.13 = (s32[128]{0:T(128)S(1)}, s32[128]{0:T(128)}, u32[]{:S(2)}) copy-start(s32[128]{0:T(128)} %broadcast_add_fusion.1) | copy-start | bytes 1540
  147.4 12.3 %copy-start.14 = (pred[256]{0:T(512)(128)(4,1)S(1)}, pred[256]{0:T(512)(128)(4,1)}, u32[]{:S(2)}) copy-start(pred[256]{0:T(512)(128)(4,1)} %iota_compare_fusion.15) | copy-start | bytes 772
  147.4 12.3 %copy-start.15 = (pred[128]{0:T(512)(128)(4,1)S(1)}, pred[128]{0:T(512)(128)(4,1)}, u32[]{:S(2)}) copy-start(pred[128]{0:T(512)(128)(4,1)} %iota_compare_fusion.16) | copy-start | bytes 388
  162.9 26.4 %copy-start.10 = (s32[16]{0:T(128)S(1)}, s32[16]{0:T(128)}, u32[]{:S(2)}) copy-start(s32[16]{0:T(128)} %copy-done.9) | copy-start | bytes 196
  164.2 27.9 %copy-start.1 = (f32[16,5,4,4,256]{4,3,2,1,0:T(4,128)S(1)}, f32[16,5,4,4,256]{4,3,2,1,0:T(4,128)}, u32[]{:S(2)}) copy-start(f32[16,5,4,4,256]{4,3,2,1,0:T(4,128)} %param.18) | copy-start | bytes 3932164
